TPU v7x, 128 devices: a whole 4x4x4 slice. The times are simulated.
128 devices in a mesh: scen: 4 (over y_lo, core), space: 32 (over x, z, y_hi).
Axes of the slice: x: 4, y: 4 (y_hi: 2, y_lo: 2; y = y_hi * 2 + y_lo), z: 4, core: 2. Of those that a mesh axis runs over, the one named last changes fastest.
Arguments:
- states: bfloat16 [3, 16, 3, 256, 32, 256], P(None, 'scen', None, 'space'), may hold values from 0.049804688 to 2
- terminal_adjoint: bfloat16 [16, 3, 256, 32, 256], P('scen', None, 'space'), may hold values from -6 to 6
- log_conductivity: float32 [256, 32, 256], P('space'), may hold values from -1 to 1
- log_rate: float32 [256, 32, 256], P('space'), may hold values from -1 to 1
- well_cell: int32 [16, 8], P('scen'), may hold values from 0 to 2097151
- sample_step: int32 [16, 8], P('scen'), may hold values from 1 to 2
- well_misfit: float32 [16, 8, 3], P('scen'), may hold values from -80 to 80
Outputs:
- update: float32 [2, 256, 32, 256], P(None, 'space', 'scen')
Inputs may be any that keep to these rules, and one draw needn't show every extreme that they name: `well_cell`: a flat cell index x * 32 * 256 + z * 256 + y; wells may share a cell. `sample_step`: the reverse step at which the well's misfit enters the adjoint.
All inputs are finite; a program needn't handle non-finite values.
Results may differ from a plain program's by a relative error of at most 0.0003.
Values may be sent and summed in bfloat16 or wider, within the bound.
A program may use at most 128 MiB of HBM per device.

v0:
```python
import functools
import math

import jax
import jax.numpy as jnp
import numpy as np
from jax import lax
from jax.experimental import pallas as pl
from jax.experimental.pallas import tpu as pltpu
from jax.sharding import PartitionSpec as P

time_step = 0.05
diffusion = (1.0, 0.8, 0.1)
donor_half = 0.5
acceptor_half = 0.3
acceptor_yield = 0.5
biomass_yield = 0.4
lengths = (40.0, 24.0)
f32 = jnp.float32
bf16 = jnp.bfloat16
MESH = pl.DeviceIdType.MESH

SL = 8
NZ = 32
NY = 256
NSC = 4
NW = 8
SP = 32
NX = SL * SP
LANES = 128


def cas(rows, cols, count):
    angle = 2.0 * np.pi * (np.outer(rows, cols) % count) / count
    return np.cos(angle) + np.sin(angle)


def two_parts(table):
    high = table.astype(np.float32).astype(bf16)
    low = (table - high.astype(np.float64)).astype(np.float32).astype(bf16)
    return np.stack([high, low])


def tables():
    count = np.arange(256)
    line = cas(count, count, 256)
    small = cas(np.arange(NZ), np.arange(NZ), NZ)
    ahead = np.zeros((NZ, SL, SL, NZ))
    back = np.zeros((4, SL, 8, NZ, SL))
    for x in range(SL):
        ahead[:, x, x, :] = small
        back[:, x, :, :, x] = small.reshape(4, 8, NZ)
    return np.stack(
        [two_parts(line), two_parts(ahead.reshape(256, 256)), two_parts(back.reshape(256, 256))]
    )


def split2(value):
    high = value.astype(bf16)
    low = (value - high.astype(f32)).astype(bf16)
    return high, low


def mm(a, b):
    return jnp.dot(a, b, preferred_element_type=f32)


def table_times(table, data):
    high, low = split2(data)
    return mm(table[0], high) + mm(table[0], low) + mm(table[1], high)


def times_table(data, table):
    high, low = split2(data)
    return mm(high, table[0]) + mm(low, table[0]) + mm(high, table[1])


def kernel(
    states,
    terminal,
    log_cond,
    log_rate,
    well_cell,
    sample_step,
    well_misfit,
    tabs_hbm,
    out,
    conc,
    adj3,
    adj2,
    adj1,
    cond,
    rate,
    weight_x,
    weight_z,
    weight_y,
    total_x,
    total_z,
    total_y,
    total_r,
    change,
    change_in,
    edge_in,
    hot,
    inject,
    tabs,
    spectrum,
    grad,
    part,
    part_in,
    half,
    half_in,
    column_out,
    column,
    back_out,
    back,
    block_out,
    block,
    local_sem,
    halo_send,
    halo_recv,
    sum_send,
    sum_recv,
    a2a_send,
    a2a_recv,
    b2a_send,
    b2a_recv,
    blk_send,
    blk_recv,
):
    scen = lax.axis_index("scen")
    space = lax.axis_index("space")
    left = lax.rem(space + SP - 1, SP)
    right = lax.rem(space + 1, SP)

    local = [
        pltpu.make_async_copy(terminal, adj3.at[:, :, 1 : 1 + SL], local_sem.at[0]),
        pltpu.make_async_copy(log_cond, cond.at[1 : 1 + SL], local_sem.at[1]),
        pltpu.make_async_copy(log_rate, rate, local_sem.at[2]),
        pltpu.make_async_copy(states.at[2], conc.at[2, :, :, 1 : 1 + SL], local_sem.at[3]),
        pltpu.make_async_copy(states.at[1], conc.at[1, :, :, 1 : 1 + SL], local_sem.at[4]),
        pltpu.make_async_copy(states.at[0], conc.at[0, :, :, 1 : 1 + SL], local_sem.at[5]),
        pltpu.make_async_copy(tabs_hbm, tabs, local_sem.at[6]),
    ]
    for copy in local:
        copy.start()

    barrier = pltpu.get_barrier_semaphore()

    def greet(i, carry):
        other = lax.rem(space + i, SP)
        pl.semaphore_signal(barrier, inc=1, device_id=(scen, other), device_id_type=MESH)
        return carry

    lax.fori_loop(1, SP, greet, 0)
    for i in range(1, 4):
        other = lax.rem(scen + i, 4)
        pl.semaphore_signal(barrier, inc=1, device_id=(other, space), device_id_type=MESH)
    pl.semaphore_wait(barrier, SP - 1 + 3)

    def to_side(i, source, target, side):
        return pltpu.make_async_remote_copy(
            src_ref=source,
            dst_ref=target,
            send_sem=halo_send.at[i],
            recv_sem=halo_recv.at[i],
            device_id=(scen, side),
            device_id_type=MESH,
        )

    halo = [
        to_side(0, log_cond.at[SL - 1], cond.at[0], right),
        to_side(1, log_cond.at[0], cond.at[SL + 1], left),
        to_side(2, terminal.at[:, :, SL - 1], adj3.at[:, :, 0], right),
        to_side(3, terminal.at[:, :, 0], adj3.at[:, :, SL + 1], left),
        to_side(4, states.at[0, :, :, SL - 1], conc.at[0, :, :, 0], right),
        to_side(5, states.at[0, :, :, 0], conc.at[0, :, :, SL + 1], left),
        to_side(6, change.at[1], change_in.at[0], right),
        to_side(7, change.at[0], change_in.at[1], left),
        to_side(8, total_x.at[SL], edge_in.at[0], right),
        to_side(9, total_x.at[0], edge_in.at[1], left),
    ]
    for i in range(6):
        halo[i].start()

    nothing = jnp.zeros((NZ, NY), f32)
    for s in range(NSC):
        for sp in range(3):
            for side in (0, SL + 1):
                conc[1, s, sp, side] = nothing.astype(bf16)
                conc[2, s, sp, side] = nothing.astype(bf16)
                adj1[s, sp, side] = nothing

    def clear(x, carry):
        total_x[x] = nothing
        total_z[x] = nothing
        total_y[x] = nothing
        total_r[x] = nothing
        return carry

    lax.fori_loop(0, SL, clear, 0)
    total_x[SL] = nothing

    lane = lax.broadcasted_iota(jnp.int32, (1, 32), 1)
    row_at = lax.broadcasted_iota(jnp.int32, (NZ, 32), 0)
    well_row = lax.broadcasted_iota(jnp.int32, (NW, NY), 0)
    well_col = lax.broadcasted_iota(jnp.int32, (NW, NY), 1)
    for s in range(NSC):
        row_of = jnp.full((1, 32), -1, jnp.int32)
        for w in range(NW):
            row = ((well_cell[s, w] - space * (SL * NZ * NY)) >> 8) + NZ
            row_of = jnp.where(lane % NW == w, row, row_of)
        row_of = jnp.where(lane < 3 * NW, row_of, -1)
        for x in range(SL + 2):
            hot[s, x] = jnp.where(row_at + x * NZ == row_of, 1.0, 0.0).astype(bf16)
        for n in (1, 2):
            for sp in range(3):
                value = jnp.zeros((NW, NY), f32)
                for w in range(NW):
                    amount = jnp.where(sample_step[s, w] == n, well_misfit[s, w, sp], 0.0)
                    here = (well_row == w) & (well_col == (well_cell[s, w] & 255))
                    value = jnp.where(here, amount, value)
                high = value.astype(bf16).astype(f32)
                rest = value - high
                middle = rest.astype(bf16).astype(f32)
                low = rest - middle
                inject[n, s, sp] = jnp.concatenate(
                    [high, middle, low, jnp.zeros((NW, NY), f32)], axis=0
                ).astype(bf16)

    local[1].wait()
    local[2].wait()
    z_index = lax.broadcasted_iota(jnp.int32, (NZ, NY), 0)
    y_index = lax.broadcasted_iota(jnp.int32, (NZ, NY), 1)

    def own_weights(x, carry):
        here = jnp.exp(cond[x])
        cond[x] = here
        rate[x - 1] = jnp.exp(rate[x - 1])
        above = jnp.sqrt(here * pltpu.roll(here, NZ - 1, 0))
        above = jnp.where(z_index == NZ - 1, 0.0, above)
        beside = jnp.sqrt(here * pltpu.roll(here, NY - 1, 1))
        beside = jnp.where(y_index == NY - 1, 0.0, beside)
        for sp in range(3):
            weight_z[sp, x - 1] = (time_step * diffusion[sp]) * above
            weight_y[sp, x - 1] = (time_step * diffusion[sp]) * beside
        return carry

    lax.fori_loop(1, SL + 1, own_weights, 0)

    def inner_weights(x, carry):
        between = jnp.sqrt(cond[x] * cond[x + 1])
        for sp in range(3):
            weight_x[sp, x] = (time_step * diffusion[sp]) * between
        return carry

    lax.fori_loop(1, SL, inner_weights, 0)

    def left_flux(adj, s, sp, x):
        here = adj[s, sp, x].astype(f32)
        return weight_x[sp, x - 1] * (here - adj[s, sp, x - 1].astype(f32))

    def layer(n, adj, new, s, x, side=None):
        own = x - 1
        conc_here = [conc[n, s, sp, x].astype(f32) for sp in range(3)]
        adj_here = [adj[s, sp, x].astype(f32) for sp in range(3)]
        sum_x = total_x[x]
        sum_z = total_z[own]
        sum_y = total_y[own]
        spread = []
        for sp in range(3):
            a, c = adj_here[sp], conc_here[sp]
            flux_x = weight_x[sp, x] * (adj[s, sp, x + 1].astype(f32) - a)
            flux_z = weight_z[sp, own] * (pltpu.roll(a, NZ - 1, 0) - a)
            flux_y = weight_y[sp, own] * (pltpu.roll(a, NY - 1, 1) - a)
            sum_x = sum_x + (conc[n, s, sp, x + 1].astype(f32) - c) * flux_x
            sum_z = sum_z + (pltpu.roll(c, NZ - 1, 0) - c) * flux_z
            sum_y = sum_y + (pltpu.roll(c, NY - 1, 1) - c) * flux_y
            if new is not None:
                spread.append(
                    (flux_x - left_flux(adj, s, sp, x))
                    + (flux_z - pltpu.roll(flux_z, 1, 0))
                    + (flux_y - pltpu.roll(flux_y, 1, 1))
                )
        total_x[x] = sum_x
        total_z[own] = sum_z
        total_y[own] = sum_y
        donor, acceptor, biomass = conc_here
        donor_inv = 1.0 / (donor_half + donor)
        accept_inv = 1.0 / (acceptor_half + acceptor)
        donor_mono = donor * donor_inv
        accept_mono = acceptor * accept_inv
        both = donor_mono * accept_mono
        stoich = -adj_here[0] - acceptor_yield * adj_here[1] + biomass_yield * adj_here[2]
        scaled = (time_step * stoich) * rate[own]
        growth = scaled * biomass
        total_r[own] = total_r[own] + growth * both
        if new is None:
            return
        spread[0] = spread[0] + (growth * accept_mono) * (donor_half * (donor_inv * donor_inv))
        spread[1] = spread[1] + (growth * donor_mono) * (acceptor_half * (accept_inv * accept_inv))
        spread[2] = spread[2] + scaled * both
        rows = hot[s, x]
        for sp in range(3):
            if side is not None:
                change[side, s, sp] = spread[sp].astype(bf16)
            new[s, sp, x] = adj_here[sp] + spread[sp] + mm(rows, inject[n, s, sp])

    def left_face(n, adj):
        def one(s, carry):
            sum_x = total_x[0]
            for sp in range(3):
                step_c = conc[n, s, sp, 1].astype(f32) - conc[n, s, sp, 0].astype(f32)
                sum_x = sum_x + step_c * left_flux(adj, s, sp, 1)
            total_x[0] = sum_x
            return carry

        lax.fori_loop(0, NSC, one, 0)

    def layers(n, adj, new, first, last):
        def one(i, carry):
            layer(n, adj, new, lax.rem(i, NSC), first + i // NSC)
            return carry

        lax.fori_loop(0, (last - first) * NSC, one, 0)

    def edges(n, adj, new, send):
        for side, x in ((0, 1), (1, SL)):

            def one(s, carry):
                layer(n, adj, new, s, x, side if send else None)
                return carry

            lax.fori_loop(0, NSC, one, 0)

    local[0].wait()
    local[3].wait()
    layers(2, adj3, adj2, 2, SL)
    for i in range(4):
        halo[i].wait_recv()
    no_left = space == 0
    no_right = space == SP - 1
    between = jnp.sqrt(jnp.exp(cond[0]) * cond[1])
    between = jnp.where(no_left, 0.0, between)
    for sp in range(3):
        weight_x[sp, 0] = (time_step * diffusion[sp]) * between
    between = jnp.sqrt(cond[SL] * jnp.exp(cond[SL + 1]))
    between = jnp.where(no_right, 0.0, between)
    for sp in range(3):
        weight_x[sp, SL] = (time_step * diffusion[sp]) * between
    edges(2, adj3, adj2, True)
    halo[6].start()
    halo[7].start()
    left_face(2, adj3)

    local[4].wait()
    layers(1, adj2, adj1, 2, SL)

    row = lax.broadcasted_iota(jnp.int32, (NX, LANES), 0)
    col = lax.broadcasted_iota(jnp.int32, (NX, LANES), 1)
    wave_x = jnp.minimum(row, NX - row).astype(f32) * (2.0 * math.pi / NX)
    freq_y = scen * 64 + col % 64
    wave_y = jnp.minimum(freq_y, NY - freq_y).astype(f32) * (2.0 * math.pi / NY)
    freq_z = jnp.full((1, LANES), space, jnp.int32)
    wave_z = jnp.minimum(freq_z, NZ - freq_z).astype(f32) * (2.0 * math.pi / NZ)
    field = (col // 64 + scen) % 2
    length = jnp.where(field == 0, lengths[0], lengths[1])
    square = wave_x * wave_x + wave_z * wave_z + wave_y * wave_y
    spectrum[...] = (length / jnp.sqrt(1.0 + (length * length) * square)) * (1.0 / (NX * NZ * NY))

    halo[6].wait_recv()
    halo[7].wait_recv()

    def halo_layers(s, carry):
        for side, x in ((0, 0), (1, SL + 1)):
            rows = hot[s, x]
            for sp in range(3):
                adj2[s, sp, x] = (
                    adj3[s, sp, x].astype(f32)
                    + change_in[side, s, sp].astype(f32)
                    + mm(rows, inject[2, s, sp])
                )
        return carry

    lax.fori_loop(0, NSC, halo_layers, 0)
    edges(1, adj2, adj1, False)
    left_face(1, adj2)

    local[5].wait()
    halo[4].wait_recv()
    halo[5].wait_recv()
    left_face(0, adj1)
    layers(0, adj1, None, SL, SL + 1)
    halo[8].start()
    halo[9].start()
    layers(0, adj1, None, 1, SL)

    def inner_grad(x):
        along_z = total_z[x]
        along_y = total_y[x]
        return (
            along_z + pltpu.roll(along_z, 1, 0) + along_y + pltpu.roll(along_y, 1, 1)
        )

    def gradients(x, carry):
        grad[0, x] = -0.5 * (inner_grad(x) + total_x[x] + total_x[x + 1])
        grad[1, x] = total_r[x]
        return carry

    lax.fori_loop(1, SL - 1, gradients, 0)
    halo[8].wait_recv()
    halo[9].wait_recv()
    grad[0, 0] = -0.5 * (inner_grad(0) + total_x[0] + edge_in[0] + total_x[1])
    grad[1, 0] = total_r[0]
    grad[0, SL - 1] = -0.5 * (inner_grad(SL - 1) + total_x[SL - 1] + total_x[SL] + edge_in[1])
    grad[1, SL - 1] = total_r[SL - 1]
    for copy in halo:
        copy.wait_send()

    local[6].wait()
    first = lax.broadcasted_iota(jnp.int32, (256, LANES), 1) < 64
    cond_y = times_table(grad[0].reshape(256, NY), tabs[0])
    rate_y = times_table(grad[1].reshape(256, NY), tabs[0])
    for chip in range(2):
        lanes = slice(chip * LANES, (chip + 1) * LANES)
        a = cond_y[:, lanes]
        b = pltpu.roll(rate_y[:, lanes], 64, 1)
        part[0, chip] = jnp.where(first, a, b)
        part[1, chip] = jnp.where(first, b, a)

    chip = scen // 2
    core = lax.rem(scen, 2)
    mate = (chip * 2 + 1 - core, space)
    far = ((1 - chip) * 2 + core, space)
    near_copies = []
    for i, which in enumerate((1 - chip, chip)):
        near_copies.append(
            pltpu.make_async_remote_copy(
                src_ref=part.at[1 - core, which],
                dst_ref=part_in.at[i],
                send_sem=sum_send.at[i],
                recv_sem=sum_recv.at[i],
                device_id=mate,
                device_id_type=MESH,
            )
        )
    for copy in near_copies:
        copy.start()
    near_copies[0].wait_recv()
    half[...] = part[core, 1 - chip] + part_in[0]
    far_copy = pltpu.make_async_remote_copy(
        src_ref=half,
        dst_ref=half_in,
        send_sem=sum_send.at[2],
        recv_sem=sum_recv.at[2],
        device_id=far,
        device_id_type=MESH,
    )
    far_copy.start()
    near_copies[1].wait_recv()
    mine = part[core, chip] + part_in[1]
    far_copy.wait_recv()
    mine = mine + half_in[...]

    column_out[...] = table_times(tabs[1], mine).reshape(SP, SL, LANES)

    def exchange(source, target, send, recv):
        def copy_of(i):
            other = lax.rem(space + i, SP)
            return pltpu.make_async_remote_copy(
                src_ref=source.at[other],
                dst_ref=target.at[space],
                send_sem=send.at[i],
                recv_sem=recv.at[i],
                device_id=(scen, other),
                device_id_type=MESH,
            )

        def begin(i, carry):
            copy_of(i).start()
            return carry

        def arrive(i, carry):
            copy_of(i).wait()
            return carry

        lax.fori_loop(1, SP, begin, 0)
        target[space] = source[space]
        lax.fori_loop(1, SP, arrive, 0)

    exchange(column_out, column, a2a_send, a2a_recv)
    spectral = table_times(tabs[0], column[...].reshape(NX, LANES)) * spectrum[...]
    back_out[...] = table_times(tabs[0], spectral).reshape(SP, SL, LANES)
    exchange(back_out, back, b2a_send, b2a_recv)

    block_out[...] = table_times(tabs[2], back[...].reshape(256, LANES)).reshape(4, 64, LANES)
    block_copies = []
    for i in range(1, 4):
        other = lax.rem(scen + i, 4)
        block_copies.append(
            pltpu.make_async_remote_copy(
                src_ref=block_out.at[other],
                dst_ref=block.at[scen],
                send_sem=blk_send.at[i],
                recv_sem=blk_recv.at[i],
                device_id=(other, space),
                device_id_type=MESH,
            )
        )
    for copy in block_copies:
        copy.start()
    block[scen] = block_out[scen]
    for copy in block_copies:
        copy.wait()
    for copy in near_copies:
        copy.wait_send()
    far_copy.wait_send()

    first = lax.broadcasted_iota(jnp.int32, (64, LANES), 1) < 64
    cond_f = [jnp.where(first, block[i], block[i + 1]) for i in (0, 2)]
    rate_f = [pltpu.roll(jnp.where(first, block[i + 1], block[i]), 64, 1) for i in (0, 2)]
    for field, halves in enumerate((cond_f, rate_f)):
        whole = jnp.concatenate(halves, axis=1)
        out[field] = times_table(whole, tabs[0]).reshape(SL, 8, NY)


def body(states, terminal, log_cond, log_rate, well_cell, sample_step, well_misfit):
    hbm = pl.BlockSpec(memory_space=pl.ANY)
    smem = pl.BlockSpec(memory_space=pltpu.SMEM)
    vmem = pl.BlockSpec(memory_space=pltpu.VMEM)
    dma = pltpu.SemaphoreType.DMA
    slab = (SL, NZ, NY)
    scratch = [
        pltpu.VMEM((3, NSC, 3, SL + 2, NZ, NY), bf16),
        pltpu.VMEM((NSC, 3, SL + 2, NZ, NY), bf16),
        pltpu.VMEM((NSC, 3, SL + 2, NZ, NY), f32),
        pltpu.VMEM((NSC, 3, SL + 2, NZ, NY), f32),
        pltpu.VMEM((SL + 2, NZ, NY), f32),
        pltpu.VMEM(slab, f32),
        pltpu.VMEM((3, SL + 1, NZ, NY), f32),
        pltpu.VMEM((3,) + slab, f32),
        pltpu.VMEM((3,) + slab, f32),
        pltpu.VMEM((SL + 1, NZ, NY), f32),
        pltpu.VMEM(slab, f32),
        pltpu.VMEM(slab, f32),
        pltpu.VMEM(slab, f32),
        pltpu.VMEM((2, NSC, 3, NZ, NY), bf16),
        pltpu.VMEM((2, NSC, 3, NZ, NY), bf16),
        pltpu.VMEM((2, NZ, NY), f32),
        pltpu.VMEM((NSC, SL + 2, NZ, 32), bf16),
        pltpu.VMEM((3, NSC, 3, 32, NY), bf16),
        pltpu.VMEM((3, 2, 256, 256), bf16),
        pltpu.VMEM((NX, LANES), f32),
        pltpu.VMEM((2,) + slab, f32),
        pltpu.VMEM((2, 2, 256, LANES), f32),
        pltpu.VMEM((2, 256, LANES), f32),
        pltpu.VMEM((256, LANES), f32),
        pltpu.VMEM((256, LANES), f32),
        pltpu.VMEM((SP, SL, LANES), f32),
        pltpu.VMEM((SP, SL, LANES), f32),
        pltpu.VMEM((SP, SL, LANES), f32),
        pltpu.VMEM((SP, SL, LANES), f32),
        pltpu.VMEM((4, 64, LANES), f32),
        pltpu.VMEM((4, 64, LANES), f32),
        dma((7,)),
        dma((10,)),
        dma((10,)),
        dma((3,)),
        dma((3,)),
        dma((SP,)),
        dma((SP,)),
        dma((SP,)),
        dma((SP,)),
        dma((4,)),
        dma((4,)),
    ]
    return pl.pallas_call(
        kernel,
        out_shape=jax.ShapeDtypeStruct((2, SL, 8, NY), f32),
        in_specs=[hbm, hbm, hbm, hbm, smem, smem, smem, hbm],
        out_specs=vmem,
        scratch_shapes=scratch,
        compiler_params=pltpu.CompilerParams(
            collective_id=0, has_side_effects=True, vmem_limit_bytes=60 * 1024 * 1024
        ),
    )(
        states,
        terminal,
        log_cond,
        log_rate,
        well_cell,
        sample_step,
        well_misfit,
        jnp.asarray(tables()),
    )


def solution(mesh):
    in_specs = (
        P(None, "scen", None, "space", None, None),
        P("scen", None, "space", None, None),
        P("space", None, None),
        P("space", None, None),
        P("scen", None),
        P("scen", None),
        P("scen", None, None),
    )
    out_specs = P(None, "space", "scen", None)
    return jax.shard_map(body, mesh=mesh, in_specs=in_specs, out_specs=out_specs, check_vma=False)
```

profile of v0, /device:TPU:1, one launch (start us, length us, event | category | flops | bytes accessed | tf_op | source)
XLA Modules:
  0.0 82.1 jit_solution(18317211985593426384)
XLA Ops:
  0.0 1.4 %copy.9.well_misfit = f32[4,8,3]{2,1,0:T(8,128)} copy(f32[4,8,3]{1,0,2:T(4,128)} %param.14) | data formatting | bytes 768 | tf_op args[6]
  1.4 79.2 %shard_map.82 = f32[2,8,8,256]{3,2,1,0:T(8,128)} custom-call(bf16[3,4,3,8,32,256]{5,4,3,2,1,0:T(8,128)(2,1)} %states.1, bf16[4,3,8,32,256]{4,3,2,1,0:T(8,128)(2,1)} %terminal.1, f32[8,32,256]{2,1,0:T(8,128)} %log_cond.1, f32[8,32,256]{2,1,0:T(8,128)} %log_rate.1, s32[4,8]{1,0:T(4,128)} %well_cell.1, s32[4,8]{1,0:T(4,128)} %sample_step.1, ...), custom_call_target="tpu_custom_call" | custom-call | tf_op jit(solution)/shard_map/pallas_call | solution.py:577
  80.6 1.6 %copy.11 = f32[2,8,8,256]{3,2,1,0:T(8,128)} copy(f32[2,8,8,256]{3,2,1,0:T(8,128)} %shard_map.82) | data formatting | bytes 262144
where the time goes:
time: 82.4 us; the launch traced here: 82.1 us
  Pallas kernels  79.2 us (96%)
  local copies, waits for them, and re-layouts  2.96 us (4%)
    pallas_call x1, Pallas kernels, body(): pl.pallas_call(kernel, out_shape=jax.ShapeDtypeStruct((2, SL, 8, NY), f32...  79.2 us
    unnamed x2, local copies, waits for them, and re-layouts  2.96 us

commit v1 on v0

v1 whole, which is shorter than its diff:
```python
import functools
import math

import jax
import jax.numpy as jnp
import numpy as np
from jax import lax
from jax.experimental import pallas as pl
from jax.experimental.pallas import tpu as pltpu
from jax.sharding import PartitionSpec as P

time_step = 0.05
diffusion = (1.0, 0.8, 0.1)
donor_half = 0.5
acceptor_half = 0.3
acceptor_yield = 0.5
biomass_yield = 0.4
lengths = (40.0, 24.0)
f32 = jnp.float32
bf16 = jnp.bfloat16
MESH = pl.DeviceIdType.MESH

SL = 8
NZ = 32
NY = 256
NSC = 4
NW = 8
SP = 32
NX = SL * SP
LANES = 128


def cas(rows, cols, count):
    angle = 2.0 * np.pi * (np.outer(rows, cols) % count) / count
    return np.cos(angle) + np.sin(angle)


def two_parts(table):
    high = table.astype(np.float32).astype(bf16)
    low = (table - high.astype(np.float64)).astype(np.float32).astype(bf16)
    return np.stack([high, low])


def tables():
    count = np.arange(256)
    line = cas(count, count, 256)
    small = cas(np.arange(NZ), np.arange(NZ), NZ)
    ahead = np.zeros((NZ, SL, SL, NZ))
    back = np.zeros((4, SL, 8, NZ, SL))
    for x in range(SL):
        ahead[:, x, x, :] = small
        back[:, x, :, :, x] = small.reshape(4, 8, NZ)
    corner = np.zeros((256, 256))
    corner[:NZ, :NZ] = small
    turned = [line, ahead.reshape(256, 256), back.reshape(256, 256), corner]
    return np.stack([two_parts(table) for table in turned])


def split2(value):
    high = value.astype(bf16)
    low = (value - high.astype(f32)).astype(bf16)
    return high, low


def mm(a, b):
    return jnp.dot(a, b, preferred_element_type=f32)


def table_times(table, data):
    high, low = split2(data)
    return mm(table[0], high) + mm(table[0], low) + mm(table[1], high)


def times_table(data, table):
    high, low = split2(data)
    return mm(high, table[0]) + mm(low, table[0]) + mm(high, table[1])


def kernel(
    states,
    terminal,
    log_cond,
    log_rate,
    well_cell,
    sample_step,
    misfit_hbm,
    tabs_hbm,
    out,
    conc,
    adj3,
    adj2,
    adj1,
    cond,
    rate,
    weight_x,
    weight_z,
    weight_y,
    total_x,
    total_z,
    total_y,
    total_r,
    change,
    change_in,
    misfit,
    hot,
    inject,
    tabs,
    spectrum,
    grad,
    part,
    part_in,
    rim,
    rim_in,
    column_out,
    column,
    back_out,
    back,
    block_out,
    block,
    local_sem,
    halo_send,
    halo_recv,
    sum_send,
    sum_recv,
    a2a_send,
    a2a_recv,
    b2a_send,
    b2a_recv,
    blk_send,
    blk_recv,
):
    scen = lax.axis_index("scen")
    space = lax.axis_index("space")
    chip = scen // 2
    core = lax.rem(scen, 2)
    left = lax.rem(space + SP - 1, SP)
    right = lax.rem(space + 1, SP)

    local = [
        pltpu.make_async_copy(terminal, adj3.at[:, :, 1 : 1 + SL], local_sem.at[0]),
        pltpu.make_async_copy(log_cond, cond.at[1 : 1 + SL], local_sem.at[1]),
        pltpu.make_async_copy(log_rate, rate, local_sem.at[2]),
        pltpu.make_async_copy(misfit_hbm, misfit, local_sem.at[3]),
        pltpu.make_async_copy(states.at[2], conc.at[2, :, :, 1 : 1 + SL], local_sem.at[4]),
        pltpu.make_async_copy(states.at[1], conc.at[1, :, :, 1 : 1 + SL], local_sem.at[5]),
        pltpu.make_async_copy(states.at[0], conc.at[0, :, :, 1 : 1 + SL], local_sem.at[6]),
        pltpu.make_async_copy(tabs_hbm, tabs, local_sem.at[7]),
    ]
    for copy in local:
        copy.start()

    barrier = pltpu.get_barrier_semaphore()

    def signal(to_scen, to_space):
        pl.semaphore_signal(
            barrier, inc=1, device_id=(to_scen, to_space), device_id_type=MESH
        )

    def greet(i, carry):
        other = lax.rem(space + i, SP)
        signal(scen, other)
        signal((1 - chip) * 2 + core, other)
        return carry

    signal((1 - chip) * 2 + core, space)
    signal(chip * 2 + 1 - core, space)
    signal((1 - chip) * 2 + 1 - core, space)
    lax.fori_loop(1, SP, greet, 0)
    pl.semaphore_wait(barrier, 2 * (SP - 1) + 3)

    def to_side(i, source, target, side):
        return pltpu.make_async_remote_copy(
            src_ref=source,
            dst_ref=target,
            send_sem=halo_send.at[i],
            recv_sem=halo_recv.at[i],
            device_id=(scen, side),
            device_id_type=MESH,
        )

    def cond_halo():
        return (
            to_side(0, log_cond.at[SL - 1], cond.at[0], right),
            to_side(1, log_cond.at[0], cond.at[SL + 1], left),
        )

    def adj_halo(s):
        return (
            to_side(2 + s, terminal.at[s, :, SL - 1], adj3.at[s, :, 0], right),
            to_side(6 + s, terminal.at[s, :, 0], adj3.at[s, :, SL + 1], left),
        )

    def change_halo(s):
        return (
            to_side(10 + s, change.at[1, s], change_in.at[0, s], right),
            to_side(14 + s, change.at[0, s], change_in.at[1, s], left),
        )

    def conc_halo(s):
        return (
            to_side(18 + s, states.at[0, s, :, SL - 1], conc.at[0, s, :, 0], right),
            to_side(22 + s, states.at[0, s, :, 0], conc.at[0, s, :, SL + 1], left),
        )

    for copy in cond_halo():
        copy.start()
    for s in range(NSC):
        for copy in adj_halo(s):
            copy.start()

    nothing = jnp.zeros((NZ, NY), f32)
    for s in range(NSC):
        for sp in range(3):
            for side in (0, SL + 1):
                conc[1, s, sp, side] = nothing.astype(bf16)
                conc[2, s, sp, side] = nothing.astype(bf16)
                adj1[s, sp, side] = nothing

    def clear(x, carry):
        total_x[x] = nothing
        total_z[x] = nothing
        total_y[x] = nothing
        total_r[x] = nothing
        return carry

    lax.fori_loop(0, SL, clear, 0)
    total_x[SL] = nothing

    local[1].wait()
    local[2].wait()
    z_index = lax.broadcasted_iota(jnp.int32, (NZ, NY), 0)
    y_index = lax.broadcasted_iota(jnp.int32, (NZ, NY), 1)

    def own_weights(x, carry):
        here = jnp.exp(cond[x])
        cond[x] = here
        rate[x - 1] = jnp.exp(rate[x - 1])
        above = jnp.sqrt(here * pltpu.roll(here, NZ - 1, 0))
        above = jnp.where(z_index == NZ - 1, 0.0, above)
        beside = jnp.sqrt(here * pltpu.roll(here, NY - 1, 1))
        beside = jnp.where(y_index == NY - 1, 0.0, beside)
        for sp in range(3):
            weight_z[sp, x - 1] = (time_step * diffusion[sp]) * above
            weight_y[sp, x - 1] = (time_step * diffusion[sp]) * beside
        return carry

    lax.fori_loop(1, SL + 1, own_weights, 0)

    def inner_weights(x, carry):
        between = jnp.sqrt(cond[x] * cond[x + 1])
        for sp in range(3):
            weight_x[sp, x] = (time_step * diffusion[sp]) * between
        return carry

    lax.fori_loop(1, SL, inner_weights, 0)

    local[3].wait()
    lane = lax.broadcasted_iota(jnp.int32, (1, 32), 1)
    row_at = lax.broadcasted_iota(jnp.int32, (NZ, 32), 0)
    well_row = lax.broadcasted_iota(jnp.int32, (NW, NY), 0)
    well_col = lax.broadcasted_iota(jnp.int32, (NW, NY), 1)

    def wells(s, carry):
        row_of = jnp.full((1, 32), -1, jnp.int32)
        col_of = jnp.zeros((NW, NY), jnp.int32)
        step_of = jnp.zeros((NW, NY), jnp.int32)
        for w in range(NW):
            cell = well_cell[s, w]
            row = ((cell - space * (SL * NZ * NY)) >> 8) + NZ
            row_of = jnp.where(lane % NW == w, row, row_of)
            col_of = jnp.where(well_row == w, cell & 255, col_of)
            step_of = jnp.where(well_row == w, sample_step[s, w], step_of)
        row_of = jnp.where(lane < 3 * NW, row_of, -1)
        for x in range(SL + 2):
            hot[s, x] = jnp.where(row_at + x * NZ == row_of, 1.0, 0.0).astype(bf16)
        here = well_col == col_of
        amount = misfit[s]
        for n in (1, 2):
            chosen = here & (step_of == n)
            for sp in range(3):
                value = jnp.where(chosen, amount[:, sp : sp + 1], 0.0)
                high = value.astype(bf16).astype(f32)
                rest = value - high
                middle = rest.astype(bf16).astype(f32)
                low = rest - middle
                inject[n, s, sp] = jnp.concatenate(
                    [high, middle, low, jnp.zeros((NW, NY), f32)], axis=0
                ).astype(bf16)
        return carry

    lax.fori_loop(0, NSC, wells, 0)

    def x_flux(adj, s, sp, x):
        before = adj[s, sp, x].astype(f32)
        return weight_x[sp, x] * (adj[s, sp, x + 1].astype(f32) - before)

    def layer(n, adj, new, s, x, side=None, face=True):
        own = x - 1
        conc_here = [conc[n, s, sp, x].astype(f32) for sp in range(3)]
        adj_here = [adj[s, sp, x].astype(f32) for sp in range(3)]
        sum_x = total_x[x]
        sum_z = total_z[own]
        sum_y = total_y[own]
        spread = []
        for sp in range(3):
            a, c = adj_here[sp], conc_here[sp]
            flux_z = weight_z[sp, own] * (pltpu.roll(a, NZ - 1, 0) - a)
            flux_y = weight_y[sp, own] * (pltpu.roll(a, NY - 1, 1) - a)
            sum_z = sum_z + (pltpu.roll(c, NZ - 1, 0) - c) * flux_z
            sum_y = sum_y + (pltpu.roll(c, NY - 1, 1) - c) * flux_y
            if face:
                flux_x = x_flux(adj, s, sp, x)
                sum_x = sum_x + (conc[n, s, sp, x + 1].astype(f32) - c) * flux_x
            if new is not None:
                spread.append(
                    (flux_x - x_flux(adj, s, sp, x - 1))
                    + (flux_z - pltpu.roll(flux_z, 1, 0))
                    + (flux_y - pltpu.roll(flux_y, 1, 1))
                )
        if face:
            total_x[x] = sum_x
        total_z[own] = sum_z
        total_y[own] = sum_y
        donor, acceptor, biomass = conc_here
        donor_inv = 1.0 / (donor_half + donor)
        accept_inv = 1.0 / (acceptor_half + acceptor)
        donor_mono = donor * donor_inv
        accept_mono = acceptor * accept_inv
        both = donor_mono * accept_mono
        stoich = -adj_here[0] - acceptor_yield * adj_here[1] + biomass_yield * adj_here[2]
        scaled = (time_step * stoich) * rate[own]
        growth = scaled * biomass
        total_r[own] = total_r[own] + growth * both
        if new is None:
            return
        spread[0] = spread[0] + (growth * accept_mono) * (donor_half * (donor_inv * donor_inv))
        spread[1] = spread[1] + (growth * donor_mono) * (acceptor_half * (accept_inv * accept_inv))
        spread[2] = spread[2] + scaled * both
        rows = hot[s, x]
        for sp in range(3):
            if side is not None:
                change[side, s, sp] = spread[sp].astype(bf16)
            new[s, sp, x] = adj_here[sp] + spread[sp] + mm(rows, inject[n, s, sp])

    def x_face(n, adj, s, x):
        total = total_x[x]
        for sp in range(3):
            step_c = conc[n, s, sp, x + 1].astype(f32) - conc[n, s, sp, x].astype(f32)
            total = total + step_c * x_flux(adj, s, sp, x)
        total_x[x] = total

    def layers(n, adj, new, s, first, last):
        def one(x, carry):
            layer(n, adj, new, s, x)
            return carry

        lax.fori_loop(first, last, one, 0)

    local[0].wait()
    local[4].wait()

    def inner_two(s, carry):
        layers(2, adj3, adj2, s, 2, SL)
        return carry

    lax.fori_loop(0, NSC, inner_two, 0)
    for copy in cond_halo():
        copy.wait_recv()
    for x, beyond, wall in ((0, 0, space == 0), (SL, SL + 1, space == SP - 1)):
        between = jnp.sqrt(jnp.exp(cond[beyond]) * cond[2 * x + 1 - beyond])
        between = jnp.where(wall, 0.0, between)
        for sp in range(3):
            weight_x[sp, x] = (time_step * diffusion[sp]) * between
    local[5].wait()

    def two_and_one(s, carry):
        for copy in adj_halo(s):
            copy.wait_recv()
        layer(2, adj3, adj2, s, 1, 0)
        layer(2, adj3, adj2, s, SL, 1)
        for copy in change_halo(s):
            copy.start()
        x_face(2, adj3, s, 0)
        layers(1, adj2, adj1, s, 2, SL)
        return carry

    lax.fori_loop(0, NSC, two_and_one, 0)
    for s in range(NSC):
        for copy in conc_halo(s):
            copy.start()

    row = lax.broadcasted_iota(jnp.int32, (NX, LANES), 0)
    col = lax.broadcasted_iota(jnp.int32, (NX, LANES), 1)
    wave_x = jnp.minimum(row, NX - row).astype(f32) * (2.0 * math.pi / NX)
    freq_y = scen * 64 + col % 64
    wave_y = jnp.minimum(freq_y, NY - freq_y).astype(f32) * (2.0 * math.pi / NY)
    freq_z = jnp.full((1, LANES), space, jnp.int32)
    wave_z = jnp.minimum(freq_z, NZ - freq_z).astype(f32) * (2.0 * math.pi / NZ)
    field = (col // 64 + scen) % 2
    length = jnp.where(field == 0, lengths[0], lengths[1])
    square = wave_x * wave_x + wave_z * wave_z + wave_y * wave_y
    spectrum[...] = (length / jnp.sqrt(1.0 + (length * length) * square)) * (1.0 / (NX * NZ * NY))
    local[6].wait()

    def one_and_none(s, carry):
        for copy in change_halo(s):
            copy.wait_recv()
        for side, x in ((0, 0), (1, SL + 1)):
            rows = hot[s, x]
            for sp in range(3):
                adj2[s, sp, x] = (
                    adj3[s, sp, x].astype(f32)
                    + change_in[side, s, sp].astype(f32)
                    + mm(rows, inject[2, s, sp])
                )
        layer(1, adj2, adj1, s, 1)
        layer(1, adj2, adj1, s, SL)
        x_face(1, adj2, s, 0)
        layers(0, adj1, None, s, 1, SL)
        layer(0, adj1, None, s, SL, face=False)
        return carry

    lax.fori_loop(0, NSC, one_and_none, 0)

    def gradients(x, carry):
        along_z = total_z[x]
        along_y = total_y[x]
        total = along_z + pltpu.roll(along_z, 1, 0) + along_y + pltpu.roll(along_y, 1, 1)
        before = jnp.where(x == 0, 0.0, total_x[x])
        after = jnp.where(x == SL - 1, 0.0, total_x[x + 1])
        grad[0, x] = -0.5 * (total + before + after)
        grad[1, x] = total_r[x]
        return carry

    lax.fori_loop(0, SL, gradients, 0)

    local[7].wait()
    first = lax.broadcasted_iota(jnp.int32, (256, LANES), 1) < 64
    cond_y = times_table(grad[0].reshape(256, NY), tabs[0])
    rate_y = times_table(grad[1].reshape(256, NY), tabs[0])
    for i in range(2):
        lanes = slice(i * LANES, (i + 1) * LANES)
        a = cond_y[:, lanes]
        b = pltpu.roll(rate_y[:, lanes], 64, 1)
        part[0, i] = jnp.where(first, a, b)
        part[1, i] = jnp.where(first, b, a)

    def to_mate(i, source, target):
        return pltpu.make_async_remote_copy(
            src_ref=source,
            dst_ref=target,
            send_sem=sum_send.at[i],
            recv_sem=sum_recv.at[i],
            device_id=(chip * 2 + 1 - core, space),
            device_id_type=MESH,
        )

    part_copy = to_mate(0, part.at[1 - core], part_in)
    part_copy.start()
    part_copy.wait_recv()
    for i in range(2):
        done = table_times(tabs[1], part[core, i] + part_in[i])
        column_out[i, :, 0:SL, :] = done.reshape(SP, SL, LANES)

    def none_faces(s, carry):
        for copy in conc_halo(s):
            copy.wait_recv()
        x_face(0, adj1, s, 0)
        x_face(0, adj1, s, SL)
        return carry

    lax.fori_loop(0, NSC, none_faces, 0)
    faces = jnp.concatenate([total_x[0], total_x[SL]], axis=0) * -0.5
    faces_y = times_table(faces, tabs[0])
    first_rim = lax.broadcasted_iota(jnp.int32, (NZ, LANES), 1) < 64
    for i in range(2):
        lanes = slice(i * LANES, (i + 1) * LANES)
        a = faces_y[0:NZ, lanes]
        b = pltpu.roll(faces_y[NZ : 2 * NZ, lanes], 64, 1)
        rim[0, i] = jnp.where(first_rim, a, b)
        rim[1, i] = jnp.where(first_rim, b, a)
    rim_copy = to_mate(1, rim.at[1 - core], rim_in)
    rim_copy.start()
    rim_copy.wait_recv()
    for i in range(2):
        done = table_times(tabs[3, :, 0:NZ, 0:NZ], rim[core, i] + rim_in[i])
        column_out[i, :, SL : SL + 1, :] = done.reshape(SP, 1, LANES)

    def column_copy(away, i):
        there = lax.rem(chip + away, 2)
        other = lax.rem(space + i, SP)
        return pltpu.make_async_remote_copy(
            src_ref=column_out.at[there, other],
            dst_ref=column.at[chip, space],
            send_sem=a2a_send.at[away, i],
            recv_sem=a2a_recv.at[away, i],
            device_id=(there * 2 + core, other),
            device_id_type=MESH,
        )

    def column_start(i, carry):
        column_copy(0, i).start()
        column_copy(1, i).start()
        return carry

    def column_wait(i, carry):
        column_copy(0, i).wait()
        column_copy(1, i).wait()
        return carry

    lax.fori_loop(1, SP, column_start, 0)
    column_copy(1, 0).start()
    column[chip, space] = column_out[chip, space]
    lax.fori_loop(1, SP, column_wait, 0)
    column_copy(1, 0).wait()
    both = column[0] + column[1]
    field_lanes = lax.broadcasted_iota(jnp.int32, (SP, 1, LANES), 2) // 64 == core
    edge = both[:, SL : SL + 1, :]
    lower = jnp.where(field_lanes, edge, 0.0)
    upper = jnp.where(field_lanes, pltpu.roll(edge.reshape(SP, LANES), 64, 1).reshape(SP, 1, LANES), 0.0)
    at_start = lower + jnp.concatenate([upper[SP - 1 :], upper[: SP - 1]], axis=0)
    at_end = upper + jnp.concatenate([lower[1:], lower[:1]], axis=0)
    place = lax.broadcasted_iota(jnp.int32, (SP, SL, LANES), 1)
    cells = both[:, 0:SL, :]
    cells = cells + jnp.where(place == 0, at_start, 0.0) + jnp.where(place == SL - 1, at_end, 0.0)

    spectral = table_times(tabs[0], cells.reshape(NX, LANES)) * spectrum[...]
    back_out[...] = table_times(tabs[0], spectral).reshape(SP, SL, LANES)

    def back_copy(i):
        other = lax.rem(space + i, SP)
        return pltpu.make_async_remote_copy(
            src_ref=back_out.at[other],
            dst_ref=back.at[space],
            send_sem=b2a_send.at[i],
            recv_sem=b2a_recv.at[i],
            device_id=(scen, other),
            device_id_type=MESH,
        )

    def back_start(i, carry):
        back_copy(i).start()
        return carry

    def back_wait(i, carry):
        back_copy(i).wait()
        return carry

    lax.fori_loop(1, SP, back_start, 0)
    back[space] = back_out[space]
    lax.fori_loop(1, SP, back_wait, 0)

    block_out[...] = table_times(tabs[2], back[...].reshape(256, LANES)).reshape(4, 64, LANES)
    block_copies = []
    for i in range(1, 4):
        other = lax.rem(scen + i, 4)
        block_copies.append(
            pltpu.make_async_remote_copy(
                src_ref=block_out.at[other],
                dst_ref=block.at[scen],
                send_sem=blk_send.at[i],
                recv_sem=blk_recv.at[i],
                device_id=(other, space),
                device_id_type=MESH,
            )
        )
    for copy in block_copies:
        copy.start()
    block[scen] = block_out[scen]
    for copy in cond_halo() + (part_copy, rim_copy):
        copy.wait_send()
    for s in range(NSC):
        for copy in adj_halo(s) + change_halo(s) + conc_halo(s):
            copy.wait_send()
    for copy in block_copies:
        copy.wait()

    first = lax.broadcasted_iota(jnp.int32, (64, LANES), 1) < 64
    cond_f = [jnp.where(first, block[i], block[i + 1]) for i in (0, 2)]
    rate_f = [pltpu.roll(jnp.where(first, block[i + 1], block[i]), 64, 1) for i in (0, 2)]
    for which, halves in enumerate((cond_f, rate_f)):
        whole = jnp.concatenate(halves, axis=1)
        out[which] = times_table(whole, tabs[0]).reshape(SL, 8, NY)


def body(states, terminal, log_cond, log_rate, well_cell, sample_step, well_misfit):
    hbm = pl.BlockSpec(memory_space=pl.ANY)
    smem = pl.BlockSpec(memory_space=pltpu.SMEM)
    vmem = pl.BlockSpec(memory_space=pltpu.VMEM)
    dma = pltpu.SemaphoreType.DMA
    slab = (SL, NZ, NY)
    scratch = [
        pltpu.VMEM((3, NSC, 3, SL + 2, NZ, NY), bf16),
        pltpu.VMEM((NSC, 3, SL + 2, NZ, NY), bf16),
        pltpu.VMEM((NSC, 3, SL + 2, NZ, NY), f32),
        pltpu.VMEM((NSC, 3, SL + 2, NZ, NY), f32),
        pltpu.VMEM((SL + 2, NZ, NY), f32),
        pltpu.VMEM(slab, f32),
        pltpu.VMEM((3, SL + 1, NZ, NY), f32),
        pltpu.VMEM((3,) + slab, f32),
        pltpu.VMEM((3,) + slab, f32),
        pltpu.VMEM((SL + 1, NZ, NY), f32),
        pltpu.VMEM(slab, f32),
        pltpu.VMEM(slab, f32),
        pltpu.VMEM(slab, f32),
        pltpu.VMEM((2, NSC, 3, NZ, NY), bf16),
        pltpu.VMEM((2, NSC, 3, NZ, NY), bf16),
        pltpu.VMEM((NSC, NW, 3), f32),
        pltpu.VMEM((NSC, SL + 2, NZ, 32), bf16),
        pltpu.VMEM((3, NSC, 3, 32, NY), bf16),
        pltpu.VMEM((4, 2, 256, 256), bf16),
        pltpu.VMEM((NX, LANES), f32),
        pltpu.VMEM((2,) + slab, f32),
        pltpu.VMEM((2, 2, 256, LANES), f32),
        pltpu.VMEM((2, 256, LANES), f32),
        pltpu.VMEM((2, 2, NZ, LANES), f32),
        pltpu.VMEM((2, NZ, LANES), f32),
        pltpu.VMEM((2, SP, SL + 1, LANES), f32),
        pltpu.VMEM((2, SP, SL + 1, LANES), f32),
        pltpu.VMEM((SP, SL, LANES), f32),
        pltpu.VMEM((SP, SL, LANES), f32),
        pltpu.VMEM((4, 64, LANES), f32),
        pltpu.VMEM((4, 64, LANES), f32),
        dma((8,)),
        dma((26,)),
        dma((26,)),
        dma((2,)),
        dma((2,)),
        dma((2, SP)),
        dma((2, SP)),
        dma((SP,)),
        dma((SP,)),
        dma((4,)),
        dma((4,)),
    ]
    return pl.pallas_call(
        kernel,
        out_shape=jax.ShapeDtypeStruct((2, SL, 8, NY), f32),
        in_specs=[hbm, hbm, hbm, hbm, smem, smem, hbm, hbm],
        out_specs=vmem,
        scratch_shapes=scratch,
        compiler_params=pltpu.CompilerParams(
            collective_id=0, has_side_effects=True, vmem_limit_bytes=60 * 1024 * 1024
        ),
    )(
        states,
        terminal,
        log_cond,
        log_rate,
        well_cell,
        sample_step,
        well_misfit,
        jnp.asarray(tables()),
    )


def solution(mesh):
    in_specs = (
        P(None, "scen", None, "space", None, None),
        P("scen", None, "space", None, None),
        P("space", None, None),
        P("space", None, None),
        P("scen", None),
        P("scen", None),
        P("scen", None, None),
    )
    out_specs = P(None, "space", "scen", None)
    return jax.shard_map(body, mesh=mesh, in_specs=in_specs, out_specs=out_specs, check_vma=False)
```

time: 82.4 us -> 66.6 us (0.81)
  Pallas kernels: 79.2 us -> 63.5 us
    pallas_call x1, Pallas kernels: 79.2 us -> 63.5 us  [body(): pl.pallas_call(kernel, out_shape=jax.ShapeDtypeStruct((2, SL, 8, NY), f32...]
where the time goes in v1:
time: 66.6 us; the launch traced here: 66.4 us
  Pallas kernels  63.5 us (95%)
  local copies, waits for them, and re-layouts  2.96 us (4%)
    pallas_call x1, Pallas kernels, body(): pl.pallas_call(kernel, out_shape=jax.ShapeDtypeStruct((2, SL, 8, NY), f32...  63.5 us
    unnamed x2, local copies, waits for them, and re-layouts  2.96 us

profile of v1, /device:TPU:1, one launch (start us, length us, event | category | flops | bytes accessed | tf_op | source)
XLA Modules:
  0.0 66.4 jit_solution(16378856936551406429)
XLA Ops:
  0.0 1.4 %copy.9.misfit_hbm = f32[4,8,3]{2,1,0:T(8,128)} copy(f32[4,8,3]{1,0,2:T(4,128)} %param.14) | data formatting | bytes 768 | tf_op args[6]
  1.4 63.5 %shard_map.82 = f32[2,8,8,256]{3,2,1,0:T(8,128)} custom-call(bf16[3,4,3,8,32,256]{5,4,3,2,1,0:T(8,128)(2,1)} %states.1, bf16[4,3,8,32,256]{4,3,2,1,0:T(8,128)(2,1)} %terminal.1, f32[8,32,256]{2,1,0:T(8,128)} %log_cond.1, f32[8,32,256]{2,1,0:T(8,128)} %log_rate.1, s32[4,8]{1,0:T(4,128)} %well_cell.1, s32[4,8]{1,0:T(4,128)} %sample_step.1, ...), custom_call_target="tpu_custom_call" | custom-call | tf_op jit(solution)/shard_map/pallas_call | solution.py:636
  64.9 1.6 %copy.11 = f32[2,8,8,256]{3,2,1,0:T(8,128)} copy(f32[2,8,8,256]{3,2,1,0:T(8,128)} %shard_map.82) | data formatting | bytes 262144

commit v2 on v1

--- a/solution.py
+++ b/solution.py
@@ -56,6 +56,17 @@
     return np.stack([two_parts(table) for table in turned])
 
 
+def offsets_of(chips):
+    found = []
+    for away in range(chips):
+        for i in range(SP):
+            x, z, y = i // 8, i // 2 % 4, i % 2
+            hops = min(x, 4 - x) + min(z, 4 - z) + (1 if away else 2 * y)
+            if hops:
+                found.append((-hops, i, away, (x, z, y)))
+    return [(away, offset) for _, _, away, offset in sorted(found)]
+
+
 def split2(value):
     high = value.astype(bf16)
     low = (value - high.astype(f32)).astype(bf16)
@@ -83,7 +94,7 @@
     log_rate,
     well_cell,
     sample_step,
-    misfit_hbm,
+    well_misfit,
     tabs_hbm,
     out,
     conc,
@@ -101,7 +112,6 @@
     total_r,
     change,
     change_in,
-    misfit,
     hot,
     inject,
     tabs,
@@ -140,15 +150,22 @@
         pltpu.make_async_copy(terminal, adj3.at[:, :, 1 : 1 + SL], local_sem.at[0]),
         pltpu.make_async_copy(log_cond, cond.at[1 : 1 + SL], local_sem.at[1]),
         pltpu.make_async_copy(log_rate, rate, local_sem.at[2]),
-        pltpu.make_async_copy(misfit_hbm, misfit, local_sem.at[3]),
-        pltpu.make_async_copy(states.at[2], conc.at[2, :, :, 1 : 1 + SL], local_sem.at[4]),
-        pltpu.make_async_copy(states.at[1], conc.at[1, :, :, 1 : 1 + SL], local_sem.at[5]),
-        pltpu.make_async_copy(states.at[0], conc.at[0, :, :, 1 : 1 + SL], local_sem.at[6]),
-        pltpu.make_async_copy(tabs_hbm, tabs, local_sem.at[7]),
+        pltpu.make_async_copy(states.at[2], conc.at[2, :, :, 1 : 1 + SL], local_sem.at[3]),
+        pltpu.make_async_copy(states.at[1], conc.at[1, :, :, 1 : 1 + SL], local_sem.at[4]),
+        pltpu.make_async_copy(states.at[0], conc.at[0, :, :, 1 : 1 + SL], local_sem.at[5]),
+        pltpu.make_async_copy(tabs_hbm, tabs, local_sem.at[6]),
     ]
     for copy in local:
         copy.start()
 
+    part_x = [lax.rem(space // 8 + i, 4) * 8 for i in range(4)]
+    part_z = [lax.rem(space // 2 + i, 4) * 2 for i in range(4)]
+    part_y = [lax.rem(space + i, 2) for i in range(2)]
+    on_chip = [chip * 2 + core, (1 - chip) * 2 + core]
+
+    def other_of(offset):
+        return part_x[offset[0]] + part_z[offset[1]] + part_y[offset[2]]
+
     barrier = pltpu.get_barrier_semaphore()
 
     def signal(to_scen, to_space):
@@ -156,16 +173,10 @@
             barrier, inc=1, device_id=(to_scen, to_space), device_id_type=MESH
         )
 
-    def greet(i, carry):
-        other = lax.rem(space + i, SP)
-        signal(scen, other)
-        signal((1 - chip) * 2 + core, other)
-        return carry
-
-    signal((1 - chip) * 2 + core, space)
+    for away, offset in offsets_of(2):
+        signal(on_chip[away], other_of(offset))
     signal(chip * 2 + 1 - core, space)
     signal((1 - chip) * 2 + 1 - core, space)
-    lax.fori_loop(1, SP, greet, 0)
     pl.semaphore_wait(barrier, 2 * (SP - 1) + 3)
 
     def to_side(i, source, target, side):
@@ -254,7 +265,6 @@
 
     lax.fori_loop(1, SL, inner_weights, 0)
 
-    local[3].wait()
     lane = lax.broadcasted_iota(jnp.int32, (1, 32), 1)
     row_at = lax.broadcasted_iota(jnp.int32, (NZ, 32), 0)
     well_row = lax.broadcasted_iota(jnp.int32, (NW, NY), 0)
@@ -264,21 +274,24 @@
         row_of = jnp.full((1, 32), -1, jnp.int32)
         col_of = jnp.zeros((NW, NY), jnp.int32)
         step_of = jnp.zeros((NW, NY), jnp.int32)
+        amounts = [jnp.zeros((NW, NY), f32)] * 3
         for w in range(NW):
             cell = well_cell[s, w]
             row = ((cell - space * (SL * NZ * NY)) >> 8) + NZ
             row_of = jnp.where(lane % NW == w, row, row_of)
             col_of = jnp.where(well_row == w, cell & 255, col_of)
             step_of = jnp.where(well_row == w, sample_step[s, w], step_of)
+            amounts = [
+                jnp.where(well_row == w, well_misfit[sp, s, w], amounts[sp]) for sp in range(3)
+            ]
         row_of = jnp.where(lane < 3 * NW, row_of, -1)
         for x in range(SL + 2):
             hot[s, x] = jnp.where(row_at + x * NZ == row_of, 1.0, 0.0).astype(bf16)
         here = well_col == col_of
-        amount = misfit[s]
         for n in (1, 2):
             chosen = here & (step_of == n)
             for sp in range(3):
-                value = jnp.where(chosen, amount[:, sp : sp + 1], 0.0)
+                value = jnp.where(chosen, amounts[sp], 0.0)
                 high = value.astype(bf16).astype(f32)
                 rest = value - high
                 middle = rest.astype(bf16).astype(f32)
@@ -357,7 +370,7 @@
         lax.fori_loop(first, last, one, 0)
 
     local[0].wait()
-    local[4].wait()
+    local[3].wait()
 
     def inner_two(s, carry):
         layers(2, adj3, adj2, s, 2, SL)
@@ -371,7 +384,7 @@
         between = jnp.where(wall, 0.0, between)
         for sp in range(3):
             weight_x[sp, x] = (time_step * diffusion[sp]) * between
-    local[5].wait()
+    local[4].wait()
 
     def two_and_one(s, carry):
         for copy in adj_halo(s):
@@ -385,10 +398,6 @@
         return carry
 
     lax.fori_loop(0, NSC, two_and_one, 0)
-    for s in range(NSC):
-        for copy in conc_halo(s):
-            copy.start()
-
     row = lax.broadcasted_iota(jnp.int32, (NX, LANES), 0)
     col = lax.broadcasted_iota(jnp.int32, (NX, LANES), 1)
     wave_x = jnp.minimum(row, NX - row).astype(f32) * (2.0 * math.pi / NX)
@@ -400,7 +409,7 @@
     length = jnp.where(field == 0, lengths[0], lengths[1])
     square = wave_x * wave_x + wave_z * wave_z + wave_y * wave_y
     spectrum[...] = (length / jnp.sqrt(1.0 + (length * length) * square)) * (1.0 / (NX * NZ * NY))
-    local[6].wait()
+    local[5].wait()
 
     def one_and_none(s, carry):
         for copy in change_halo(s):
@@ -413,6 +422,8 @@
                     + change_in[side, s, sp].astype(f32)
                     + mm(rows, inject[2, s, sp])
                 )
+        for copy in conc_halo(s):
+            copy.start()
         layer(1, adj2, adj1, s, 1)
         layer(1, adj2, adj1, s, SL)
         x_face(1, adj2, s, 0)
@@ -434,7 +445,7 @@
 
     lax.fori_loop(0, SL, gradients, 0)
 
-    local[7].wait()
+    local[6].wait()
     first = lax.broadcasted_iota(jnp.int32, (256, LANES), 1) < 64
     cond_y = times_table(grad[0].reshape(256, NY), tabs[0])
     rate_y = times_table(grad[1].reshape(256, NY), tabs[0])
@@ -486,33 +497,25 @@
         done = table_times(tabs[3, :, 0:NZ, 0:NZ], rim[core, i] + rim_in[i])
         column_out[i, :, SL : SL + 1, :] = done.reshape(SP, 1, LANES)
 
-    def column_copy(away, i):
-        there = lax.rem(chip + away, 2)
-        other = lax.rem(space + i, SP)
-        return pltpu.make_async_remote_copy(
-            src_ref=column_out.at[there, other],
-            dst_ref=column.at[chip, space],
-            send_sem=a2a_send.at[away, i],
-            recv_sem=a2a_recv.at[away, i],
-            device_id=(there * 2 + core, other),
-            device_id_type=MESH,
-        )
-
-    def column_start(i, carry):
-        column_copy(0, i).start()
-        column_copy(1, i).start()
-        return carry
-
-    def column_wait(i, carry):
-        column_copy(0, i).wait()
-        column_copy(1, i).wait()
-        return carry
-
-    lax.fori_loop(1, SP, column_start, 0)
-    column_copy(1, 0).start()
+    column_copies = []
+    for i, (away, offset) in enumerate(offsets_of(2)):
+        there = chip if away == 0 else 1 - chip
+        other = other_of(offset)
+        column_copies.append(
+            pltpu.make_async_remote_copy(
+                src_ref=column_out.at[there, other],
+                dst_ref=column.at[chip, space],
+                send_sem=a2a_send.at[i],
+                recv_sem=a2a_recv.at[i],
+                device_id=(on_chip[away], other),
+                device_id_type=MESH,
+            )
+        )
+    for copy in column_copies:
+        copy.start()
     column[chip, space] = column_out[chip, space]
-    lax.fori_loop(1, SP, column_wait, 0)
-    column_copy(1, 0).wait()
+    for copy in column_copies:
+        copy.wait_recv()
     both = column[0] + column[1]
     field_lanes = lax.broadcasted_iota(jnp.int32, (SP, 1, LANES), 2) // 64 == core
     edge = both[:, SL : SL + 1, :]
@@ -527,28 +530,24 @@
     spectral = table_times(tabs[0], cells.reshape(NX, LANES)) * spectrum[...]
     back_out[...] = table_times(tabs[0], spectral).reshape(SP, SL, LANES)
 
-    def back_copy(i):
-        other = lax.rem(space + i, SP)
-        return pltpu.make_async_remote_copy(
-            src_ref=back_out.at[other],
-            dst_ref=back.at[space],
-            send_sem=b2a_send.at[i],
-            recv_sem=b2a_recv.at[i],
-            device_id=(scen, other),
-            device_id_type=MESH,
-        )
-
-    def back_start(i, carry):
-        back_copy(i).start()
-        return carry
-
-    def back_wait(i, carry):
-        back_copy(i).wait()
-        return carry
-
-    lax.fori_loop(1, SP, back_start, 0)
+    back_copies = []
+    for i, (_, offset) in enumerate(offsets_of(1)):
+        other = other_of(offset)
+        back_copies.append(
+            pltpu.make_async_remote_copy(
+                src_ref=back_out.at[other],
+                dst_ref=back.at[space],
+                send_sem=b2a_send.at[i],
+                recv_sem=b2a_recv.at[i],
+                device_id=(scen, other),
+                device_id_type=MESH,
+            )
+        )
+    for copy in back_copies:
+        copy.start()
     back[space] = back_out[space]
-    lax.fori_loop(1, SP, back_wait, 0)
+    for copy in back_copies:
+        copy.wait_recv()
 
     block_out[...] = table_times(tabs[2], back[...].reshape(256, LANES)).reshape(4, 64, LANES)
     block_copies = []
@@ -568,6 +567,8 @@
         copy.start()
     block[scen] = block_out[scen]
     for copy in cond_halo() + (part_copy, rim_copy):
+        copy.wait_send()
+    for copy in column_copies + back_copies:
         copy.wait_send()
     for s in range(NSC):
         for copy in adj_halo(s) + change_halo(s) + conc_halo(s):
@@ -605,7 +606,6 @@
         pltpu.VMEM(slab, f32),
         pltpu.VMEM((2, NSC, 3, NZ, NY), bf16),
         pltpu.VMEM((2, NSC, 3, NZ, NY), bf16),
-        pltpu.VMEM((NSC, NW, 3), f32),
         pltpu.VMEM((NSC, SL + 2, NZ, 32), bf16),
         pltpu.VMEM((3, NSC, 3, 32, NY), bf16),
         pltpu.VMEM((4, 2, 256, 256), bf16),
@@ -621,22 +621,22 @@
         pltpu.VMEM((SP, SL, LANES), f32),
         pltpu.VMEM((4, 64, LANES), f32),
         pltpu.VMEM((4, 64, LANES), f32),
-        dma((8,)),
+        dma((7,)),
         dma((26,)),
         dma((26,)),
         dma((2,)),
         dma((2,)),
-        dma((2, SP)),
-        dma((2, SP)),
-        dma((SP,)),
-        dma((SP,)),
+        dma((2 * SP - 1,)),
+        dma((2 * SP - 1,)),
+        dma((SP - 1,)),
+        dma((SP - 1,)),
         dma((4,)),
         dma((4,)),
     ]
     return pl.pallas_call(
         kernel,
         out_shape=jax.ShapeDtypeStruct((2, SL, 8, NY), f32),
-        in_specs=[hbm, hbm, hbm, hbm, smem, smem, hbm, hbm],
+        in_specs=[hbm, hbm, hbm, hbm, smem, smem, smem, hbm],
         out_specs=vmem,
         scratch_shapes=scratch,
         compiler_params=pltpu.CompilerParams(
@@ -649,7 +649,7 @@
         log_rate,
         well_cell,
         sample_step,
-        well_misfit,
+        jnp.transpose(well_misfit, (2, 0, 1)),
         jnp.asarray(tables()),
     )
 

time: 66.6 us -> 63.1 us (0.947)
  Pallas kernels: 63.5 us -> 61.3 us
  local copies, waits for them, and re-layouts: 2.96 us -> 1.57 us
    pallas_call x1, Pallas kernels: 63.5 us -> 61.3 us  [body(): pl.pallas_call(kernel, out_shape=jax.ShapeDtypeStruct((2, SL, 8, NY), f32...]
    unnamed x2 -> x1, local copies, waits for them, and re-layouts: 2.96 us -> 1.57 us
where the time goes in v2:
time: 63.1 us; the launch traced here: 62.9 us
  Pallas kernels  61.3 us (97%)
  local copies, waits for them, and re-layouts  1.57 us (2%)
    pallas_call x1, Pallas kernels, body(): pl.pallas_call(kernel, out_shape=jax.ShapeDtypeStruct((2, SL, 8, NY), f32...  61.3 us
    unnamed x1, local copies, waits for them, and re-layouts  1.57 us

profile of v2, /device:TPU:1, one launch (start us, length us, event | category | flops | bytes accessed | tf_op | source)
XLA Modules:
  0.0 62.9 jit_solution(14913116754392410776)
XLA Ops:
  0.0 61.3 %shard_map.82 = f32[2,8,8,256]{3,2,1,0:T(8,128)} custom-call(bf16[3,4,3,8,32,256]{5,4,3,2,1,0:T(8,128)(2,1)} %states.1, bf16[4,3,8,32,256]{4,3,2,1,0:T(8,128)(2,1)} %terminal.1, f32[8,32,256]{2,1,0:T(8,128)} %log_cond.1, f32[8,32,256]{2,1,0:T(8,128)} %log_rate.1, s32[4,8]{1,0:T(4,128)} %well_cell.1, s32[4,8]{1,0:T(4,128)} %sample_step.1, ...), custom_call_target="tpu_custom_call" | custom-call | tf_op jit(solution)/shard_map/pallas_call | solution.py:636
  61.3 1.6 %copy.10 = f32[2,8,8,256]{3,2,1,0:T(8,128)} copy(f32[2,8,8,256]{3,2,1,0:T(8,128)} %shard_map.82) | data formatting | bytes 262144

commit v3 on v2

--- a/solution.py
+++ b/solution.py
@@ -576,16 +576,20 @@
     for copy in block_copies:
         copy.wait()
 
+    out[...] = block[...]
+
+
+def along_y(block, tabs, out):
     first = lax.broadcasted_iota(jnp.int32, (64, LANES), 1) < 64
     cond_f = [jnp.where(first, block[i], block[i + 1]) for i in (0, 2)]
     rate_f = [pltpu.roll(jnp.where(first, block[i + 1], block[i]), 64, 1) for i in (0, 2)]
     for which, halves in enumerate((cond_f, rate_f)):
         whole = jnp.concatenate(halves, axis=1)
-        out[which] = times_table(whole, tabs[0]).reshape(SL, 8, NY)
+        out[which] = times_table(whole, tabs).reshape(SL, 8, NY)
 
 
 def body(states, terminal, log_cond, log_rate, well_cell, sample_step, well_misfit):
-    hbm = pl.BlockSpec(memory_space=pl.ANY)
+    hbm = pl.BlockSpec(memory_space=pltpu.HBM)
     smem = pl.BlockSpec(memory_space=pltpu.SMEM)
     vmem = pl.BlockSpec(memory_space=pltpu.VMEM)
     dma = pltpu.SemaphoreType.DMA
@@ -633,25 +637,34 @@
         dma((4,)),
         dma((4,)),
     ]
-    return pl.pallas_call(
+    blocks = pl.pallas_call(
         kernel,
-        out_shape=jax.ShapeDtypeStruct((2, SL, 8, NY), f32),
+        out_shape=jax.ShapeDtypeStruct((4, 64, LANES), f32),
         in_specs=[hbm, hbm, hbm, hbm, smem, smem, smem, hbm],
         out_specs=vmem,
         scratch_shapes=scratch,
         compiler_params=pltpu.CompilerParams(
-            collective_id=0, has_side_effects=True, vmem_limit_bytes=60 * 1024 * 1024
+            collective_id=0, has_side_effects=True, vmem_limit_bytes=40 * 1024 * 1024
         ),
     )(
-        states,
-        terminal,
-        log_cond,
-        log_rate,
-        well_cell,
-        sample_step,
-        jnp.transpose(well_misfit, (2, 0, 1)),
-        jnp.asarray(tables()),
+        *[
+            pltpu.with_memory_space_constraint(value, pltpu.HBM)
+            for value in (states, terminal, log_cond, log_rate)
+        ],
+        *[
+            pltpu.with_memory_space_constraint(value, pltpu.HBM)
+            for value in (well_cell, sample_step, jnp.transpose(well_misfit, (2, 0, 1)))
+        ],
+        pltpu.with_memory_space_constraint(jnp.asarray(tables()), pltpu.HBM),
     )
+    line = jnp.asarray(two_parts(cas(np.arange(256), np.arange(256), 256)))
+    return pl.pallas_call(
+        along_y,
+        out_shape=jax.ShapeDtypeStruct((2, SL, 8, NY), f32),
+        in_specs=[vmem, vmem],
+        out_specs=vmem,
+        compiler_params=pltpu.CompilerParams(vmem_limit_bytes=8 * 1024 * 1024),
+    )(blocks, line)
 
 
 def solution(mesh):

time: 63.1 us -> 61.6 us (0.976)
  local copies, waits for them, and re-layouts: 1.57 us -> 0.01 us
    unnamed x1 -> x2, local copies, waits for them, and re-layouts: 1.57 us -> 0.01 us
    pallas_call x1 -> x2, Pallas kernels: 61.3 us -> 61.5 us  [the longest x1 60.5 us: body(): pl.pallas_call(kernel, out_shape=jax.ShapeDtypeStruct((4, 64, LANES), f32...]
where the time goes in v3:
time: 61.6 us; the launch traced here: 61.5 us
  Pallas kernels  61.5 us (100%)
    pallas_call x1, Pallas kernels, body(): pl.pallas_call(kernel, out_shape=jax.ShapeDtypeStruct((4, 64, LANES), f32...  60.5 us

profile of v3, /device:TPU:1, one launch (start us, length us, event | category | flops | bytes accessed | tf_op | source)
XLA Modules:
  0.0 61.5 jit_solution(18277003708774487201)
XLA Ops:
  0.0 0.0 copy-start
  0.0 60.5 %shard_map.91.block = f32[4,64,128]{2,1,0:T(8,128)S(1)} custom-call(bf16[3,4,3,8,32,256]{5,4,3,2,1,0:T(8,128)(2,1)} %states.1, bf16[4,3,8,32,256]{4,3,2,1,0:T(8,128)(2,1)} %terminal.1, f32[8,32,256]{2,1,0:T(8,128)} %log_cond.1, f32[8,32,256]{2,1,0:T(8,128)} %log_rate.1, s32[4,8]{1,0:T(4,128)} %well_cell.1, s32[4,8]{1,0:T(4,128)} %sample_step.1, ...), custom_call_target="tpu_custom_call" | custom-call | tf_op jit(solution)/shard_map/pallas_call | solution.py:640
  60.6 0.0 copy-done
  60.6 0.9 %shard_map.92 = f32[2,8,8,256]{3,2,1,0:T(8,128)} custom-call(f32[4,64,128]{2,1,0:T(8,128)S(1)} %shard_map.91.block, bf16[2,256,256]{2,1,0:T(8,128)(2,1)S(1)} %copy-done), custom_call_target="tpu_custom_call" | custom-call | tf_op jit(solution)/shard_map/pallas_call | solution.py:661
Async XLA Ops:
  0.0 60.6 %copy-start = (bf16[2,256,256]{2,1,0:T(8,128)(2,1)S(1)}, bf16[2,256,256]{2,1,0:T(8,128)(2,1)}, u32[]{:S(2)}) copy-start(bf16[2,256,256]{2,1,0:T(8,128)(2,1)} %constant.5.clone.tabs) | copy-start | bytes 786436

commit v4 on v3

--- a/solution.py
+++ b/solution.py
@@ -53,7 +53,14 @@
     corner = np.zeros((256, 256))
     corner[:NZ, :NZ] = small
     turned = [line, ahead.reshape(256, 256), back.reshape(256, 256), corner]
-    return np.stack([two_parts(table) for table in turned])
+    next_y = np.eye(NY, k=-1) - np.eye(NY)
+    next_y[:, -1] = 0.0
+    next_z = np.eye(NZ, k=1) - np.eye(NZ)
+    next_z[-1] = 0.0
+    three = np.zeros((256, 256))
+    three[: 3 * NZ, : 3 * NZ] = np.kron(np.eye(3), next_z)
+    steps = np.stack([next_y, three]).astype(np.float32).astype(bf16)
+    return np.stack([two_parts(table) for table in turned] + [steps])
 
 
 def offsets_of(chips):
@@ -92,9 +99,9 @@
     terminal,
     log_cond,
     log_rate,
-    well_cell,
-    sample_step,
-    well_misfit,
+    cell_hbm,
+    sample_hbm,
+    misfit_hbm,
     tabs_hbm,
     out,
     conc,
@@ -112,8 +119,12 @@
     total_r,
     change,
     change_in,
+    well_cell,
+    sample_step,
+    well_misfit,
     hot,
     inject,
+    flux,
     tabs,
     spectrum,
     grad,
@@ -154,9 +165,12 @@
         pltpu.make_async_copy(states.at[1], conc.at[1, :, :, 1 : 1 + SL], local_sem.at[4]),
         pltpu.make_async_copy(states.at[0], conc.at[0, :, :, 1 : 1 + SL], local_sem.at[5]),
         pltpu.make_async_copy(tabs_hbm, tabs, local_sem.at[6]),
+        pltpu.make_async_copy(cell_hbm, well_cell, local_sem.at[7]),
+        pltpu.make_async_copy(sample_hbm, sample_step, local_sem.at[8]),
+        pltpu.make_async_copy(misfit_hbm, well_misfit, local_sem.at[9]),
     ]
-    for copy in local:
-        copy.start()
+    for i in (1, 2, 7, 8, 9, 0, 3, 6, 4, 5):
+        local[i].start()
 
     part_x = [lax.rem(space // 8 + i, 4) * 8 for i in range(4)]
     part_z = [lax.rem(space // 2 + i, 4) * 2 for i in range(4)]
@@ -265,6 +279,8 @@
 
     lax.fori_loop(1, SL, inner_weights, 0)
 
+    for i in (7, 8, 9):
+        local[i].wait()
     lane = lax.broadcasted_iota(jnp.int32, (1, 32), 1)
     row_at = lax.broadcasted_iota(jnp.int32, (NZ, 32), 0)
     well_row = lax.broadcasted_iota(jnp.int32, (NW, NY), 0)
@@ -296,37 +312,58 @@
                 rest = value - high
                 middle = rest.astype(bf16).astype(f32)
                 low = rest - middle
-                inject[n, s, sp] = jnp.concatenate(
+                inject[n, s, :, sp * NY : (sp + 1) * NY] = jnp.concatenate(
                     [high, middle, low, jnp.zeros((NW, NY), f32)], axis=0
                 ).astype(bf16)
         return carry
 
     lax.fori_loop(0, NSC, wells, 0)
 
-    def x_flux(adj, s, sp, x):
-        before = adj[s, sp, x].astype(f32)
-        return weight_x[sp, x] * (adj[s, sp, x + 1].astype(f32) - before)
+    def x_face(n, adj, s, x, keep=False):
+        total = total_x[x]
+        for sp in range(3):
+            step_a = adj[s, sp, x + 1].astype(f32) - adj[s, sp, x].astype(f32)
+            step_c = conc[n, s, sp, x + 1].astype(f32) - conc[n, s, sp, x].astype(f32)
+            through = weight_x[sp, x] * step_a
+            total = total + step_c * through
+            if keep:
+                flux[s, sp, x] = through
+        total_x[x] = total
+
+    def injected(n, s, x):
+        added = mm(hot[s, x], inject[n, s])
+        return [added[:, sp * NY : (sp + 1) * NY] for sp in range(3)]
 
     def layer(n, adj, new, s, x, side=None, face=True):
         own = x - 1
+        three = conc[n, s, :, x].reshape(3 * NZ, NY)
+        steps_y = mm(three, tabs[4, 0])
+        steps_z = mm(tabs[4, 1, 0 : 3 * NZ, 0 : 3 * NZ], three)
         conc_here = [conc[n, s, sp, x].astype(f32) for sp in range(3)]
         adj_here = [adj[s, sp, x].astype(f32) for sp in range(3)]
-        sum_x = total_x[x]
         sum_z = total_z[own]
         sum_y = total_y[own]
+        if face:
+            sum_x = total_x[x]
         spread = []
         for sp in range(3):
-            a, c = adj_here[sp], conc_here[sp]
+            a = adj_here[sp]
+            rows = slice(sp * NZ, (sp + 1) * NZ)
             flux_z = weight_z[sp, own] * (pltpu.roll(a, NZ - 1, 0) - a)
             flux_y = weight_y[sp, own] * (pltpu.roll(a, NY - 1, 1) - a)
-            sum_z = sum_z + (pltpu.roll(c, NZ - 1, 0) - c) * flux_z
-            sum_y = sum_y + (pltpu.roll(c, NY - 1, 1) - c) * flux_y
+            sum_z = sum_z + steps_z[rows] * flux_z
+            sum_y = sum_y + steps_y[rows] * flux_y
             if face:
-                flux_x = x_flux(adj, s, sp, x)
-                sum_x = sum_x + (conc[n, s, sp, x + 1].astype(f32) - c) * flux_x
+                flux_x = weight_x[sp, x] * (adj[s, sp, x + 1].astype(f32) - a)
+                step_c = conc[n, s, sp, x + 1].astype(f32) - conc_here[sp]
+                sum_x = sum_x + step_c * flux_x
+                if new is not None:
+                    flux[s, sp, x] = flux_x
+            elif new is not None:
+                flux_x = flux[s, sp, x]
             if new is not None:
                 spread.append(
-                    (flux_x - x_flux(adj, s, sp, x - 1))
+                    (flux_x - flux[s, sp, x - 1])
                     + (flux_z - pltpu.roll(flux_z, 1, 0))
                     + (flux_y - pltpu.roll(flux_y, 1, 1))
                 )
@@ -349,31 +386,35 @@
         spread[0] = spread[0] + (growth * accept_mono) * (donor_half * (donor_inv * donor_inv))
         spread[1] = spread[1] + (growth * donor_mono) * (acceptor_half * (accept_inv * accept_inv))
         spread[2] = spread[2] + scaled * both
-        rows = hot[s, x]
+        added = injected(n, s, x)
         for sp in range(3):
             if side is not None:
                 change[side, s, sp] = spread[sp].astype(bf16)
-            new[s, sp, x] = adj_here[sp] + spread[sp] + mm(rows, inject[n, s, sp])
-
-    def x_face(n, adj, s, x):
-        total = total_x[x]
-        for sp in range(3):
-            step_c = conc[n, s, sp, x + 1].astype(f32) - conc[n, s, sp, x].astype(f32)
-            total = total + step_c * x_flux(adj, s, sp, x)
-        total_x[x] = total
+            new[s, sp, x] = adj_here[sp] + spread[sp] + added[sp]
 
     def layers(n, adj, new, s, first, last):
-        def one(x, carry):
-            layer(n, adj, new, s, x)
+        def two(i, carry):
+            layer(n, adj, new, s, first + 2 * i)
+            layer(n, adj, new, s, first + 2 * i + 1)
             return carry
 
-        lax.fori_loop(first, last, one, 0)
+        lax.fori_loop(0, (last - first) // 2, two, 0)
+
+    def inner(n, adj, new, s):
+        x_face(n, adj, s, 1, True)
+        layers(n, adj, new, s, 2, SL)
+
+    def outer(n, adj, new, s, sides=(None, None)):
+        x_face(n, adj, s, 0, True)
+        layer(n, adj, new, s, 1, sides[0], face=False)
+        layer(n, adj, new, s, SL, sides[1])
 
     local[0].wait()
     local[3].wait()
+    local[6].wait()
 
     def inner_two(s, carry):
-        layers(2, adj3, adj2, s, 2, SL)
+        inner(2, adj3, adj2, s)
         return carry
 
     lax.fori_loop(0, NSC, inner_two, 0)
@@ -389,12 +430,10 @@
     def two_and_one(s, carry):
         for copy in adj_halo(s):
             copy.wait_recv()
-        layer(2, adj3, adj2, s, 1, 0)
-        layer(2, adj3, adj2, s, SL, 1)
+        outer(2, adj3, adj2, s, (0, 1))
         for copy in change_halo(s):
             copy.start()
-        x_face(2, adj3, s, 0)
-        layers(1, adj2, adj1, s, 2, SL)
+        inner(1, adj2, adj1, s)
         return carry
 
     lax.fori_loop(0, NSC, two_and_one, 0)
@@ -415,19 +454,16 @@
         for copy in change_halo(s):
             copy.wait_recv()
         for side, x in ((0, 0), (1, SL + 1)):
-            rows = hot[s, x]
+            added = injected(2, s, x)
             for sp in range(3):
                 adj2[s, sp, x] = (
-                    adj3[s, sp, x].astype(f32)
-                    + change_in[side, s, sp].astype(f32)
-                    + mm(rows, inject[2, s, sp])
+                    adj3[s, sp, x].astype(f32) + change_in[side, s, sp].astype(f32) + added[sp]
                 )
         for copy in conc_halo(s):
             copy.start()
-        layer(1, adj2, adj1, s, 1)
-        layer(1, adj2, adj1, s, SL)
-        x_face(1, adj2, s, 0)
-        layers(0, adj1, None, s, 1, SL)
+        outer(1, adj2, adj1, s)
+        layers(0, adj1, None, s, 1, SL - 1)
+        layer(0, adj1, None, s, SL - 1)
         layer(0, adj1, None, s, SL, face=False)
         return carry
 
@@ -445,7 +481,6 @@
 
     lax.fori_loop(0, SL, gradients, 0)
 
-    local[6].wait()
     first = lax.broadcasted_iota(jnp.int32, (256, LANES), 1) < 64
     cond_y = times_table(grad[0].reshape(256, NY), tabs[0])
     rate_y = times_table(grad[1].reshape(256, NY), tabs[0])
@@ -549,22 +584,34 @@
     for copy in back_copies:
         copy.wait_recv()
 
-    block_out[...] = table_times(tabs[2], back[...].reshape(256, LANES)).reshape(4, 64, LANES)
-    block_copies = []
-    for i in range(1, 4):
-        other = lax.rem(scen + i, 4)
-        block_copies.append(
-            pltpu.make_async_remote_copy(
-                src_ref=block_out.at[other],
-                dst_ref=block.at[scen],
-                send_sem=blk_send.at[i],
-                recv_sem=blk_recv.at[i],
-                device_id=(other, space),
-                device_id_type=MESH,
-            )
-        )
-    for copy in block_copies:
-        copy.start()
+    back_high, back_low = split2(back[...].reshape(256, LANES))
+
+    def z_blocks(which):
+        rows = pl.ds(pl.multiple_of(which * 128, 128), 128)
+        high, low = tabs[2, 0, rows, :], tabs[2, 1, rows, :]
+        done = mm(high, back_high) + mm(high, back_low) + mm(low, back_high)
+        return done.reshape(2, 64, LANES)
+
+    def block_copy(i, other):
+        return pltpu.make_async_remote_copy(
+            src_ref=block_out.at[other],
+            dst_ref=block.at[scen],
+            send_sem=blk_send.at[i],
+            recv_sem=blk_recv.at[i],
+            device_id=(other, space),
+            device_id_type=MESH,
+        )
+
+    block_copies = [
+        block_copy(1, (1 - chip) * 2 + core),
+        block_copy(2, (1 - chip) * 2 + 1 - core),
+        block_copy(3, chip * 2 + 1 - core),
+    ]
+    block_out[pl.ds((1 - chip) * 2, 2)] = z_blocks(1 - chip)
+    block_copies[0].start()
+    block_copies[1].start()
+    block_out[pl.ds(chip * 2, 2)] = z_blocks(chip)
+    block_copies[2].start()
     block[scen] = block_out[scen]
     for copy in cond_halo() + (part_copy, rim_copy):
         copy.wait_send()
@@ -590,7 +637,6 @@
 
 def body(states, terminal, log_cond, log_rate, well_cell, sample_step, well_misfit):
     hbm = pl.BlockSpec(memory_space=pltpu.HBM)
-    smem = pl.BlockSpec(memory_space=pltpu.SMEM)
     vmem = pl.BlockSpec(memory_space=pltpu.VMEM)
     dma = pltpu.SemaphoreType.DMA
     slab = (SL, NZ, NY)
@@ -610,9 +656,13 @@
         pltpu.VMEM(slab, f32),
         pltpu.VMEM((2, NSC, 3, NZ, NY), bf16),
         pltpu.VMEM((2, NSC, 3, NZ, NY), bf16),
+        pltpu.SMEM((NSC, NW), jnp.int32),
+        pltpu.SMEM((NSC, NW), jnp.int32),
+        pltpu.SMEM((3, NSC, NW), f32),
         pltpu.VMEM((NSC, SL + 2, NZ, 32), bf16),
-        pltpu.VMEM((3, NSC, 3, 32, NY), bf16),
-        pltpu.VMEM((4, 2, 256, 256), bf16),
+        pltpu.VMEM((3, NSC, 32, 3 * NY), bf16),
+        pltpu.VMEM((NSC, 3, SL + 1, NZ, NY), f32),
+        pltpu.VMEM((5, 2, 256, 256), bf16),
         pltpu.VMEM((NX, LANES), f32),
         pltpu.VMEM((2,) + slab, f32),
         pltpu.VMEM((2, 2, 256, LANES), f32),
@@ -625,7 +675,7 @@
         pltpu.VMEM((SP, SL, LANES), f32),
         pltpu.VMEM((4, 64, LANES), f32),
         pltpu.VMEM((4, 64, LANES), f32),
-        dma((7,)),
+        dma((10,)),
         dma((26,)),
         dma((26,)),
         dma((2,)),
@@ -640,7 +690,7 @@
     blocks = pl.pallas_call(
         kernel,
         out_shape=jax.ShapeDtypeStruct((4, 64, LANES), f32),
-        in_specs=[hbm, hbm, hbm, hbm, smem, smem, smem, hbm],
+        in_specs=[hbm] * 8,
         out_specs=vmem,
         scratch_shapes=scratch,
         compiler_params=pltpu.CompilerParams(

time: 61.6 us -> 60.8 us (0.987)
  Pallas kernels: 61.5 us -> 60.7 us
    pallas_call x1, Pallas kernels: 60.5 us -> 59.7 us  [body(): pl.pallas_call(kernel, out_shape=jax.ShapeDtypeStruct((4, 64, LANES), f32...]
where the time goes in v4:
time: 60.8 us; the launch traced here: 60.7 us
  Pallas kernels  60.7 us (100%)
    pallas_call x1, Pallas kernels, body(): pl.pallas_call(kernel, out_shape=jax.ShapeDtypeStruct((4, 64, LANES), f32...  59.7 us

profile of v4, /device:TPU:1, one launch (start us, length us, event | category | flops | bytes accessed | tf_op | source)
XLA Modules:
  0.0 60.7 jit_solution(18341614840651793683)
XLA Ops:
  0.0 0.0 copy-start
  0.0 59.7 %shard_map.91.block = f32[4,64,128]{2,1,0:T(8,128)S(1)} custom-call(bf16[3,4,3,8,32,256]{5,4,3,2,1,0:T(8,128)(2,1)} %states.1, bf16[4,3,8,32,256]{4,3,2,1,0:T(8,128)(2,1)} %terminal.1, f32[8,32,256]{2,1,0:T(8,128)} %log_cond.1, f32[8,32,256]{2,1,0:T(8,128)} %log_rate.1, s32[4,8]{1,0:T(4,128)} %cell_hbm.1, s32[4,8]{1,0:T(4,128)} %sample_hbm.1, ...), custom_call_target="tpu_custom_call" | custom-call | tf_op jit(solution)/shard_map/pallas_call | solution.py:690
  59.7 0.0 copy-done
  59.8 0.9 %shard_map.92 = f32[2,8,8,256]{3,2,1,0:T(8,128)} custom-call(f32[4,64,128]{2,1,0:T(8,128)S(1)} %shard_map.91.block, bf16[2,256,256]{2,1,0:T(8,128)(2,1)S(1)} %copy-done), custom_call_target="tpu_custom_call" | custom-call | tf_op jit(solution)/shard_map/pallas_call | solution.py:711
Async XLA Ops:
  0.0 59.7 %copy-start = (bf16[2,256,256]{2,1,0:T(8,128)(2,1)S(1)}, bf16[2,256,256]{2,1,0:T(8,128)(2,1)}, u32[]{:S(2)}) copy-start(bf16[2,256,256]{2,1,0:T(8,128)(2,1)} %constant.5.clone.tabs) | copy-start | bytes 786436

commit v5 on v4

--- a/solution.py
+++ b/solution.py
@@ -86,7 +86,9 @@
 
 def table_times(table, data):
     high, low = split2(data)
-    return mm(table[0], high) + mm(table[0], low) + mm(table[1], high)
+    width = data.shape[1]
+    both = mm(table[0], jnp.concatenate([high, low], axis=1))
+    return both[:, :width] + both[:, width:] + mm(table[1], high)
 
 
 def times_table(data, table):
@@ -585,11 +587,13 @@
         copy.wait_recv()
 
     back_high, back_low = split2(back[...].reshape(256, LANES))
+    back_both = jnp.concatenate([back_high, back_low], axis=1)
 
     def z_blocks(which):
         rows = pl.ds(pl.multiple_of(which * 128, 128), 128)
         high, low = tabs[2, 0, rows, :], tabs[2, 1, rows, :]
-        done = mm(high, back_high) + mm(high, back_low) + mm(low, back_high)
+        both = mm(high, back_both)
+        done = both[:, :LANES] + both[:, LANES:] + mm(low, back_high)
         return done.reshape(2, 64, LANES)
 
     def block_copy(i, other):

time: 60.8 us -> 60.6 us (level)
  no operation moved by 1% of the time
where the time goes in v5:
time: 60.6 us; the launch traced here: 60.5 us
  Pallas kernels  60.5 us (100%)
    pallas_call x1, Pallas kernels, body(): pl.pallas_call(kernel, out_shape=jax.ShapeDtypeStruct((4, 64, LANES), f32...  59.5 us

profile of v5, /device:TPU:1, one launch (start us, length us, event | category | flops | bytes accessed | tf_op | source)
XLA Modules:
  0.0 60.5 jit_solution(13497284206197437704)
XLA Ops:
  0.0 0.0 copy-start
  0.0 59.5 %shard_map.91.block = f32[4,64,128]{2,1,0:T(8,128)S(1)} custom-call(bf16[3,4,3,8,32,256]{5,4,3,2,1,0:T(8,128)(2,1)} %states.1, bf16[4,3,8,32,256]{4,3,2,1,0:T(8,128)(2,1)} %terminal.1, f32[8,32,256]{2,1,0:T(8,128)} %log_cond.1, f32[8,32,256]{2,1,0:T(8,128)} %log_rate.1, s32[4,8]{1,0:T(4,128)} %cell_hbm.1, s32[4,8]{1,0:T(4,128)} %sample_hbm.1, ...), custom_call_target="tpu_custom_call" | custom-call | tf_op jit(solution)/shard_map/pallas_call | solution.py:694
  59.5 0.0 copy-done
  59.5 0.9 %shard_map.92 = f32[2,8,8,256]{3,2,1,0:T(8,128)} custom-call(f32[4,64,128]{2,1,0:T(8,128)S(1)} %shard_map.91.block, bf16[2,256,256]{2,1,0:T(8,128)(2,1)S(1)} %copy-done), custom_call_target="tpu_custom_call" | custom-call | tf_op jit(solution)/shard_map/pallas_call | solution.py:715
Async XLA Ops:
  0.0 59.5 %copy-start = (bf16[2,256,256]{2,1,0:T(8,128)(2,1)S(1)}, bf16[2,256,256]{2,1,0:T(8,128)(2,1)}, u32[]{:S(2)}) copy-start(bf16[2,256,256]{2,1,0:T(8,128)(2,1)} %constant.5.clone.tabs) | copy-start | bytes 786436

commit v6 on v5

--- a/solution.py
+++ b/solution.py
@@ -634,9 +634,11 @@
     first = lax.broadcasted_iota(jnp.int32, (64, LANES), 1) < 64
     cond_f = [jnp.where(first, block[i], block[i + 1]) for i in (0, 2)]
     rate_f = [pltpu.roll(jnp.where(first, block[i + 1], block[i]), 64, 1) for i in (0, 2)]
-    for which, halves in enumerate((cond_f, rate_f)):
-        whole = jnp.concatenate(halves, axis=1)
-        out[which] = times_table(whole, tabs).reshape(SL, 8, NY)
+    wholes = [jnp.concatenate(halves, axis=1) for halves in (cond_f, rate_f)]
+    high, low = split2(jnp.concatenate(wholes, axis=0))
+    both = mm(jnp.concatenate([high, low], axis=0), tabs[0])
+    done = both[:128] + both[128:] + mm(high, tabs[1])
+    out[...] = done.reshape(2, SL, 8, NY)
 
 
 def body(states, terminal, log_cond, log_rate, well_cell, sample_step, well_misfit):

time: 60.6 us -> 60.5 us (level)
  no operation moved by 1% of the time
where the time goes in v6:
time: 60.5 us
  Pallas kernels  60.4 us (100%)
    pallas_call x1, Pallas kernels, body(): pl.pallas_call(kernel, out_shape=jax.ShapeDtypeStruct((4, 64, LANES), f32...  59.5 us

profile of v6, /device:TPU:1, one launch (start us, length us, event | category | flops | bytes accessed | tf_op | source)
XLA Modules:
  0.0 60.5 jit_solution(5036561268286862601)
XLA Ops:
  0.0 0.0 copy-start
  0.0 59.5 %shard_map.91.block = f32[4,64,128]{2,1,0:T(8,128)S(1)} custom-call(bf16[3,4,3,8,32,256]{5,4,3,2,1,0:T(8,128)(2,1)} %states.1, bf16[4,3,8,32,256]{4,3,2,1,0:T(8,128)(2,1)} %terminal.1, f32[8,32,256]{2,1,0:T(8,128)} %log_cond.1, f32[8,32,256]{2,1,0:T(8,128)} %log_rate.1, s32[4,8]{1,0:T(4,128)} %cell_hbm.1, s32[4,8]{1,0:T(4,128)} %sample_hbm.1, ...), custom_call_target="tpu_custom_call" | custom-call | tf_op jit(solution)/shard_map/pallas_call | solution.py:696
  59.5 0.0 copy-done
  59.5 0.9 %shard_map.92 = f32[2,8,8,256]{3,2,1,0:T(8,128)} custom-call(f32[4,64,128]{2,1,0:T(8,128)S(1)} %shard_map.91.block, bf16[2,256,256]{2,1,0:T(8,128)(2,1)S(1)} %copy-done), custom_call_target="tpu_custom_call" | custom-call | tf_op jit(solution)/shard_map/pallas_call | solution.py:717
Async XLA Ops:
  0.0 59.5 %copy-start = (bf16[2,256,256]{2,1,0:T(8,128)(2,1)S(1)}, bf16[2,256,256]{2,1,0:T(8,128)(2,1)}, u32[]{:S(2)}) copy-start(bf16[2,256,256]{2,1,0:T(8,128)(2,1)} %constant.5.clone.tabs) | copy-start | bytes 786436
